TPU v7x, 128 devices: a whole 4x4x4 slice. The times are simulated.
128 devices in a mesh: frames: 2 (over core), prow: 8 (over z_lo, x), pcol: 8 (over y, z_hi).
Axes of the slice: x: 4, y: 4, z: 4 (z_hi: 2, z_lo: 2; z = z_hi * 2 + z_lo), core: 2. Of those that a mesh axis runs over, the one named last changes fastest.
Arguments:
- poses: bfloat16 [262144, 256], P(('frames', 'prow', 'pcol')), may hold values from -6 to 6
- codebook: bfloat16 [32, 256], replicated, may hold values from -4 to 4
- offsets: bfloat16 [32, 256], replicated, may hold values from -4 to 4
- confidence: float32 [262144], P(('frames', 'prow', 'pcol')), may hold values from 0.2 to 1
- code_ids: int32 [262144], P(('frames', 'prow', 'pcol')), may hold values from 0 to 31
- creature_ids: int32 [262144], P(('frames', 'prow', 'pcol')), may hold values from 0 to 31
- hess_raw: float32 [8, 8, 128, 8, 8, 128], P(None, 'prow', None, None, 'pcol'), may hold values from -1 to 1, as said below
- pattern: int32 [64, 64], replicated, may hold values from 0 to 1, as said below
- membership: int32 [2, 2], replicated, may hold values from 0 to 63, as said below
Outputs:
- factor_state: float32 [8, 8, 128, 8, 8, 128], P(None, 'prow', None, None, 'pcol')
- reduced_grad: float32 [8, 8, 128], P(None, 'prow')
Inputs may be any that keep to these rules, and one draw needn't show every extreme that they name: As an 8192 x 8192 matrix hess_raw is symmetric. pattern is symmetric with ones on its diagonal. Within each row of membership all pattern entries are one, and for every block row i outside a supernode, pattern[i, p] is the same for all block columns p of that supernode. The 4 entries of membership are distinct block indices.
All inputs are finite; a program needn't handle non-finite values.
Results may differ from a plain program's by a relative error of at most 0.0003.
Values sent between devices are 32-bit elements; how exact they have to be, the bound alone decides.
A program may use at most 64 MiB of HBM per device.

v0:
```python
import math
import jax
import jax.numpy as jnp
from jax import lax
from jax.sharding import PartitionSpec as P

NPAN = 8192
precise = lax.Precision.HIGHEST


def from_root(value, axis, source):
    kept = jnp.where(lax.axis_index(axis) == source, value, 0).astype(value.dtype)
    return lax.psum(kept, axis)


def solve_rows(factor_blk, column):
    blocksize = factor_blk.shape[0]
    block_count = column.shape[0]
    right_side = jnp.transpose(column, (2, 0, 1)).reshape(blocksize, block_count * blocksize)
    solution = jax.scipy.linalg.solve_triangular(factor_blk, right_side, lower=True)
    return jnp.transpose(solution.reshape(blocksize, block_count, blocksize), (1, 2, 0))


def shards(
    poses, codebook, offsets, confidence, code_ids, creature_ids, hess_raw, pattern, membership
):
    grid_rows = lax.axis_size("prow")
    grid_cols = lax.axis_size("pcol")
    my_row = lax.axis_index("prow")
    my_col = lax.axis_index("pcol")
    code_count = codebook.shape[0]
    kind_count = offsets.shape[0]
    local_rows = hess_raw.shape[0]
    local_cols = hess_raw.shape[3]
    blocksize = hess_raw.shape[2]
    code_table = (code_ids[None, :] == jnp.arange(code_count, dtype=jnp.int32)[:, None]).astype(
        jnp.float32
    )
    kind_table = (creature_ids[None, :] == jnp.arange(kind_count, dtype=jnp.int32)[:, None]).astype(
        jnp.float32
    )
    predicted = jnp.einsum("cf,cw->fw", code_table, codebook.astype(jnp.float32), precision=precise)
    predicted = predicted + jnp.einsum(
        "cf,cw->fw", kind_table, offsets.astype(jnp.float32), precision=precise
    )
    residual = confidence[:, None] * (poses.astype(jnp.float32) - predicted)
    frame_total = poses.shape[0] * lax.axis_size("frames") * grid_rows * grid_cols
    partial_grad = jnp.einsum("cf,fw->cw", code_table, residual, precision=precise) / math.sqrt(
        frame_total / code_count
    )
    partial_grad = partial_grad.reshape(local_rows, grid_rows, blocksize)
    summed = lax.psum(partial_grad, ("frames", "prow", "pcol"))
    grad_local = lax.dynamic_index_in_dim(summed, my_row, 1, False)
    shift = 2.5 * math.sqrt(NPAN)
    local_pattern = pattern.reshape(local_rows, grid_rows, local_cols, grid_cols)
    local_pattern = lax.dynamic_index_in_dim(local_pattern, my_row, 1, False)
    local_pattern = lax.dynamic_index_in_dim(local_pattern, my_col, 2, False)
    mask_four = local_pattern.astype(jnp.float32)[:, None, :, None]
    row_ids = jnp.arange(local_rows, dtype=jnp.int32) * grid_rows + my_row
    col_ids = jnp.arange(local_cols, dtype=jnp.int32) * grid_cols + my_col
    same_block = (row_ids[:, None] == col_ids[None, :]).astype(jnp.float32)
    identity = jnp.eye(blocksize, dtype=jnp.float32)
    matrix = (
        hess_raw[:, 0, :, :, 0, :] * mask_four
        + shift * same_block[:, None, :, None] * identity[None, :, None, :]
    )
    order = membership.reshape(-1)

    def eliminate(position, state_pair):
        matrix, grad_local = state_pair
        pivot = order[position]
        pivot_row = pivot % grid_rows
        pivot_col = pivot % grid_cols
        slot_row = pivot // grid_rows
        slot_col = pivot // grid_cols
        on_row = my_row == pivot_row
        on_col = my_col == pivot_col
        diag_here = lax.dynamic_index_in_dim(
            lax.dynamic_index_in_dim(matrix, slot_row, 0, False), slot_col, 1, False
        )
        grad_here = lax.dynamic_index_in_dim(grad_local, slot_row, 0, False)
        diag_blk, grad_blk = (
            from_root(diag_here, ("prow", "pcol"), pivot_row * grid_cols + pivot_col),
            from_root(grad_here, ("prow", "pcol"), pivot_row * grid_cols + pivot_col),
        )
        factor_blk = jnp.linalg.cholesky(diag_blk)
        solved = jax.scipy.linalg.solve_triangular(factor_blk, grad_blk, lower=True)
        column = lax.dynamic_index_in_dim(matrix, slot_col, 2, False)
        column = column * (row_ids != pivot).astype(jnp.float32)[:, None, None]
        panel_rows = from_root(solve_rows(factor_blk, column), "pcol", pivot_col)
        mirrored = from_root(panel_rows, "prow", my_col)
        matrix = matrix - mask_four * jnp.einsum(
            "ixk,jyk->ixjy", panel_rows, mirrored, precision=precise
        )
        grad_local = grad_local - jnp.einsum("ixk,k->ix", panel_rows, solved, precision=precise)
        grad_local = jnp.where(
            on_row, lax.dynamic_update_index_in_dim(grad_local, solved, slot_row, 0), grad_local
        )
        row_block = lax.dynamic_index_in_dim(matrix, slot_row, 0, False)
        matrix = lax.dynamic_update_index_in_dim(
            matrix, jnp.where(on_row, jnp.zeros_like(row_block), row_block), slot_row, 0
        )
        col_block = lax.dynamic_index_in_dim(matrix, slot_col, 2, False)
        filled = jnp.where(
            on_row, lax.dynamic_update_index_in_dim(panel_rows, factor_blk, slot_row, 0), panel_rows
        )
        matrix = lax.dynamic_update_index_in_dim(
            matrix, jnp.where(on_col, filled, col_block), slot_col, 2
        )
        return (matrix, grad_local)

    matrix, grad_local = lax.fori_loop(0, order.shape[0], eliminate, (matrix, grad_local))
    return (matrix[:, None, :, :, None, :], grad_local[:, None, :])


def solution(mesh):
    return jax.shard_map(
        shards,
        mesh=mesh,
        in_specs=(
            P(("frames", "prow", "pcol"), None),
            P(),
            P(),
            P(("frames", "prow", "pcol")),
            P(("frames", "prow", "pcol")),
            P(("frames", "prow", "pcol")),
            P(None, "prow", None, None, "pcol", None),
            P(),
            P(),
        ),
        out_specs=(P(None, "prow", None, None, "pcol", None), P(None, "prow", None)),
        check_vma=False,
    )
```

profile of v0, /device:TPU:0, one launch (start us, length us, event | category | flops | bytes accessed | tf_op | source)
XLA Modules:
  0.0 1798.9 jit_solution(806905055227306704)
XLA Ops:
  10.4 2.0 fusion.16
  13.3 68.3 %psum.67 = f32[8,8,128]{2,1,0:T(8,128)S(1)} all-reduce(f32[8,8,128]{2,1,0:T(8,128)S(1)} %reshape.143), channel_id=1, replica_groups=mesh['frames'=2,'prow'=8,'pcol'=8] {'frames','prow','pcol'}, use_global_device_ids=true, to_apply=%region_0.0 | all-reduce | flops 8192 | bytes 65536 | tf_op jit(solution)/shard_map/psum | solution.py:52
  81.7 10.9 copy.33
  92.5 4.7 fusion.14
  97.2 1689.5 %while.20 = (s32[]{:T(128)}, f32[8,128,8,128]{1,3,2,0:T(8,128)}, f32[8,128]{1,0:T(8,128)S(1)}, f32[8,1,8,1]{2,0,3,1:T(8,128)S(1)}, s32[4]{0:T(128)S(1)}, /*index...) while((s32[]{:T(128)}, f32[8,128,8,128]{1,3,2,0:T(8,128)}, ...), condition=%wide.region_8.9_spmd.clone.clone, body=%wide.region_1.8_spmd.clone.clone.sunk | while | flops 1816970880 | bytes 44392472 | solution.py:112
  103.5 117.8 %all-reduce.4.cloned.1.call-done = f32[128,128]{0,1:T(8,128)} async-done(((f32[128,128]{0,1:T(8,128)}), f32[128,128]{0,1:T(8,128)}) %all-reduce.4.cloned.1.call-update) | async-done | bytes 65552 | tf_op jit(solution)/shard_map/while/body/eval_jaxpr/psum | solution.py:13
  223.1 11.7 cholesky.80
  236.3 9.8 custom-call.29
  247.6 5.3 copy.44
  253.0 176.0 %psum.83 = f32[128]{0:T(128)S(1)} all-reduce(f32[128]{0:T(128)S(1)} %fusion.50), channel_id=1, replica_groups=mesh['frames'=2,'prow'=8,'pcol'=8] {'prow','pcol'}, use_global_device_ids=true, to_apply=%region_7.7 | all-reduce | flops 128 | bytes 1024 | tf_op jit(solution)/shard_map/while/body/eval_jaxpr/psum | solution.py:13
  429.0 1.9 broadcast_select_fusion.5
  431.0 1.6 fusion.52
  432.7 66.4 %all-reduce.8.cloned.1.call-done = f32[8,128,128]{2,1,0:T(8,128)} async-done(((f32[8,128,128]{2,1,0:T(8,128)}), f32[8,128,128]{2,1,0:T(8,128)}) %all-reduce.8.cloned.1.call-update) | async-done | bytes 524304 | tf_op jit(solution)/shard_map/while/body/eval_jaxpr/psum | solution.py:13
  499.1 8.2 multiply_subtract_fusion.2
  507.3 1.9 select_dynamic-update-slice_fusion.2
  511.8 5.3 copy.47
  523.4 120.9 %all-reduce.4.cloned.1.call-done = f32[128,128]{0,1:T(8,128)} async-done(((f32[128,128]{0,1:T(8,128)}), f32[128,128]{0,1:T(8,128)}) %all-reduce.4.cloned.1.call-update) | async-done | bytes 65552 | tf_op jit(solution)/shard_map/while/body/eval_jaxpr/psum | solution.py:13
  646.1 11.7 cholesky.80
  659.3 9.8 custom-call.29
  670.6 5.3 copy.44
  676.0 176.0 %psum.83 = f32[128]{0:T(128)S(1)} all-reduce(f32[128]{0:T(128)S(1)} %fusion.50), channel_id=1, replica_groups=mesh['frames'=2,'prow'=8,'pcol'=8] {'prow','pcol'}, use_global_device_ids=true, to_apply=%region_7.7 | all-reduce | flops 128 | bytes 1024 | tf_op jit(solution)/shard_map/while/body/eval_jaxpr/psum | solution.py:13
  852.0 1.9 broadcast_select_fusion.5
  854.1 1.6 fusion.52
  855.8 66.4 %all-reduce.8.cloned.1.call-done = f32[8,128,128]{2,1,0:T(8,128)} async-done(((f32[8,128,128]{2,1,0:T(8,128)}), f32[8,128,128]{2,1,0:T(8,128)}) %all-reduce.8.cloned.1.call-update) | async-done | bytes 524304 | tf_op jit(solution)/shard_map/while/body/eval_jaxpr/psum | solution.py:13
  922.2 8.2 multiply_subtract_fusion.2
  930.4 1.9 select_dynamic-update-slice_fusion.2
  934.9 5.3 copy.47
  946.5 121.1 %all-reduce.4.cloned.1.call-done = f32[128,128]{0,1:T(8,128)} async-done(((f32[128,128]{0,1:T(8,128)}), f32[128,128]{0,1:T(8,128)}) %all-reduce.4.cloned.1.call-update) | async-done | bytes 65552 | tf_op jit(solution)/shard_map/while/body/eval_jaxpr/psum | solution.py:13
  1069.5 11.7 cholesky.80
  1082.6 9.8 custom-call.29
  1094.0 5.3 copy.44
  1099.3 176.0 %psum.83 = f32[128]{0:T(128)S(1)} all-reduce(f32[128]{0:T(128)S(1)} %fusion.50), channel_id=1, replica_groups=mesh['frames'=2,'prow'=8,'pcol'=8] {'prow','pcol'}, use_global_device_ids=true, to_apply=%region_7.7 | all-reduce | flops 128 | bytes 1024 | tf_op jit(solution)/shard_map/while/body/eval_jaxpr/psum | solution.py:13
  1275.3 1.9 broadcast_select_fusion.5
  1279.1 66.4 %all-reduce.8.cloned.1.call-done = f32[8,128,128]{2,1,0:T(8,128)} async-done(((f32[8,128,128]{2,1,0:T(8,128)}), f32[8,128,128]{2,1,0:T(8,128)}) %all-reduce.8.cloned.1.call-update) | async-done | bytes 524304 | tf_op jit(solution)/shard_map/while/body/eval_jaxpr/psum | solution.py:13
  1345.5 8.2 multiply_subtract_fusion.2
  1353.7 1.9 select_dynamic-update-slice_fusion.2
  1358.2 5.3 copy.47
  1369.8 120.9 %all-reduce.4.cloned.1.call-done = f32[128,128]{0,1:T(8,128)} async-done(((f32[128,128]{0,1:T(8,128)}), f32[128,128]{0,1:T(8,128)}) %all-reduce.4.cloned.1.call-update) | async-done | bytes 65552 | tf_op jit(solution)/shard_map/while/body/eval_jaxpr/psum | solution.py:13
  1492.5 11.7 cholesky.80
  1505.7 9.8 custom-call.29
  1517.0 5.3 copy.44
  1522.4 176.0 %psum.83 = f32[128]{0:T(128)S(1)} all-reduce(f32[128]{0:T(128)S(1)} %fusion.50), channel_id=1, replica_groups=mesh['frames'=2,'prow'=8,'pcol'=8] {'prow','pcol'}, use_global_device_ids=true, to_apply=%region_7.7 | all-reduce | flops 128 | bytes 1024 | tf_op jit(solution)/shard_map/while/body/eval_jaxpr/psum | solution.py:13
  1698.4 1.9 broadcast_select_fusion.5
  1702.1 66.5 %all-reduce.8.cloned.1.call-done = f32[8,128,128]{2,1,0:T(8,128)} async-done(((f32[8,128,128]{2,1,0:T(8,128)}), f32[8,128,128]{2,1,0:T(8,128)}) %all-reduce.8.cloned.1.call-update) | async-done | bytes 524304 | tf_op jit(solution)/shard_map/while/body/eval_jaxpr/psum | solution.py:13
  1768.6 8.2 multiply_subtract_fusion.2
  1776.8 1.9 select_dynamic-update-slice_fusion.2
  1781.3 5.3 copy.47
  1786.7 5.3 copy.35
  (131 shorter events, 53.7 us)
Async XLA Ops:
  7.2 2.1 copy-start
  7.2 5.2 copy-start.3
  97.2 124.1 %all-reduce.4.cloned.1.call-start = ((), (), s32[]{:S(2)}) async-start(), calls=%async_computation | async-start | bytes 131072 | tf_op jit(solution)/shard_map/while/body/eval_jaxpr/psum | solution.py:13
  101.6 327.4 %all-reduce.6.cloned.1.call-start = ((), (), s32[]{:S(2)}) async-start(), calls=%async_computation.1 | async-start | bytes 1048576 | tf_op jit(solution)/shard_map/while/body/eval_jaxpr/psum | solution.py:13
  247.5 251.6 %all-reduce.8.cloned.1.call-start = ((), (), s32[]{:S(2)}) async-start(), calls=%async_computation.2 | async-start | bytes 1048576 | tf_op jit(solution)/shard_map/while/body/eval_jaxpr/psum | solution.py:13
  499.1 11.1 copy-start.1
  517.2 127.1 %all-reduce.4.cloned.1.call-start = ((), (), s32[]{:S(2)}) async-start(), calls=%async_computation | async-start | bytes 131072 | tf_op jit(solution)/shard_map/while/body/eval_jaxpr/psum | solution.py:13
  521.5 330.5 %all-reduce.6.cloned.1.call-start = ((), (), s32[]{:S(2)}) async-start(), calls=%async_computation.1 | async-start | bytes 1048576 | tf_op jit(solution)/shard_map/while/body/eval_jaxpr/psum | solution.py:13
  670.6 251.6 %all-reduce.8.cloned.1.call-start = ((), (), s32[]{:S(2)}) async-start(), calls=%async_computation.2 | async-start | bytes 1048576 | tf_op jit(solution)/shard_map/while/body/eval_jaxpr/psum | solution.py:13
  922.2 11.1 copy-start.1
  940.2 127.4 %all-reduce.4.cloned.1.call-start = ((), (), s32[]{:S(2)}) async-start(), calls=%async_computation | async-start | bytes 131072 | tf_op jit(solution)/shard_map/while/body/eval_jaxpr/psum | solution.py:13
  944.6 330.7 %all-reduce.6.cloned.1.call-start = ((), (), s32[]{:S(2)}) async-start(), calls=%async_computation.1 | async-start | bytes 1048576 | tf_op jit(solution)/shard_map/while/body/eval_jaxpr/psum | solution.py:13
  1093.9 251.6 %all-reduce.8.cloned.1.call-start = ((), (), s32[]{:S(2)}) async-start(), calls=%async_computation.2 | async-start | bytes 1048576 | tf_op jit(solution)/shard_map/while/body/eval_jaxpr/psum | solution.py:13
  1345.5 11.1 copy-start.1
  1363.5 127.1 %all-reduce.4.cloned.1.call-start = ((), (), s32[]{:S(2)}) async-start(), calls=%async_computation | async-start | bytes 131072 | tf_op jit(solution)/shard_map/while/body/eval_jaxpr/psum | solution.py:13
  1367.9 330.5 %all-reduce.6.cloned.1.call-start = ((), (), s32[]{:S(2)}) async-start(), calls=%async_computation.1 | async-start | bytes 1048576 | tf_op jit(solution)/shard_map/while/body/eval_jaxpr/psum | solution.py:13
  1516.9 251.7 %all-reduce.8.cloned.1.call-start = ((), (), s32[]{:S(2)}) async-start(), calls=%async_computation.2 | async-start | bytes 1048576 | tf_op jit(solution)/shard_map/while/body/eval_jaxpr/psum | solution.py:13
  1768.6 11.1 copy-start.1
  1786.7 5.3 copy-start.2
Sparse Core Ops, SparseCore 0:
  103.3 117.9 all-reduce.3
  247.7 83.5 all-reduce.5
  431.0 68.0 all-reduce.7
  522.9 121.3 all-reduce.3
  670.7 83.5 all-reduce.5
  854.0 68.0 all-reduce.7
  946.3 121.2 all-reduce.3
  1094.0 83.5 all-reduce.5
  1277.4 68.0 all-reduce.7
  1369.3 121.3 all-reduce.3
  1517.1 83.5 all-reduce.5
  1700.4 68.1 all-reduce.7
where the time goes:
time: 1800 us
  blocking collectives  772 us (43%)
  waiting for transfers between devices  747 us (42%)
  other arithmetic  130 us (7%)
  local copies, waits for them, and re-layouts  76.4 us (4%)
  matrix products  49.5 us (3%)
    psum x12, waiting for transfers between devices, from_root(): return lax.psum(kept, axis)  746 us
    psum x4, blocking collectives, from_root(): return lax.psum(kept, axis)  704 us
    psum x1, blocking collectives, shards(): summed = lax.psum(partial_grad, ('frames', 'prow', 'pcol'))  68.3 us
    another operation x12, other arithmetic, eliminate(): factor_blk = jnp.linalg.cholesky(diag_blk)  49.9 us
    while x16, local copies, waits for them, and re-layouts  42.8 us
    another operation x8, other arithmetic, solve_rows(): jax.scipy.linalg.solve_triangular(factor_blk, right_side, lower=True)  42 us
  transfers between devices with their start and end apart: 12, of which 8 were waited for; matrix products, arithmetic and copies ran while one was open for 2% of the time, Pallas kernels for 0%

commit v1 on v0

--- a/solution.py
+++ b/solution.py
@@ -49,7 +49,7 @@
         frame_total / code_count
     )
     partial_grad = partial_grad.reshape(local_rows, grid_rows, blocksize)
-    summed = lax.psum(partial_grad, ("frames", "prow", "pcol"))
+    summed = jnp.sum(lax.all_gather(partial_grad, ("frames", "prow", "pcol")), axis=0)
     grad_local = lax.dynamic_index_in_dim(summed, my_row, 1, False)
     shift = 2.5 * math.sqrt(NPAN)
     local_pattern = pattern.reshape(local_rows, grid_rows, local_cols, grid_cols)

time: 1800 us -> 1920 us (1.067)
  waiting for transfers between devices: 747 us -> 934 us
  blocking collectives: 772 us -> 704 us
    all_gather x0 -> x1, waiting for transfers between devices: none -> 185 us  [shards(): lax.all_gather(partial_grad, ('frames', 'prow', 'pcol'))]
    psum x1 -> x0, blocking collectives: 68.3 us -> none  [shards(): summed = lax.psum(partial_grad, ('frames', 'prow', 'pcol'))]
  transfers between devices with their start and end apart: 12 -> 13, of which waited for: 8 -> 9; matrix products, arithmetic and copies ran while one was open for 2% -> 3% of each run, Pallas kernels for 0% -> 0%
where the time goes in v1:
time: 1920 us
  waiting for transfers between devices  934 us (49%)
  blocking collectives  704 us (37%)
  other arithmetic  131 us (7%)
  local copies, waits for them, and re-layouts  76.1 us (4%)
  matrix products  49.5 us (3%)
    psum x12, waiting for transfers between devices, from_root(): return lax.psum(kept, axis)  749 us
    psum x4, blocking collectives, from_root(): return lax.psum(kept, axis)  704 us
    all_gather x1, waiting for transfers between devices, shards(): lax.all_gather(partial_grad, ('frames', 'prow', 'pcol'))  185 us
    another operation x12, other arithmetic, eliminate(): factor_blk = jnp.linalg.cholesky(diag_blk)  49.4 us
    while x16, local copies, waits for them, and re-layouts  42.8 us
    another operation x8, other arithmetic, solve_rows(): jax.scipy.linalg.solve_triangular(factor_blk, right_side, lower=True)  41.6 us
  transfers between devices with their start and end apart: 13, of which 9 were waited for; matrix products, arithmetic and copies ran while one was open for 3% of the time, Pallas kernels for 0%

profile of v1, /device:TPU:0, one launch (start us, length us, event | category | flops | bytes accessed | tf_op | source)
XLA Modules:
  0.0 1919.2 jit_solution(5506662451103007685)
XLA Ops:
  9.1 2.0 fusion.16
  13.1 10.9 copy.42
  24.1 4.7 fusion.14
  28.8 185.0 %all-gather.2.cloned.1.call-done = f32[128,8,8,128]{3,2,1,0:T(8,128)} async-done(((f32[1,8,8,128]{3,2,1,0:T(8,128)}), f32[128,8,8,128]{3,2,1,0:T(8,128)}) %all-gather.2.cloned.1.call-update) | async-done | bytes 4194320 | tf_op jit(solution)/shard_map/all_gather | solution.py:52
  213.8 2.5 reduce_sum.9
  216.3 1691.0 %while.20 = (s32[]{:T(128)}, f32[8,128,8,128]{1,3,2,0:T(8,128)}, f32[8,128]{1,0:T(8,128)S(1)}, f32[8,1,8,1]{2,0,3,1:T(8,128)S(1)}, s32[4]{0:T(128)S(1)}, /*index...) while((s32[]{:T(128)}, f32[8,128,8,128]{1,3,2,0:T(8,128)}, ...), condition=%wide.region_8.9_spmd.clone.clone, body=%wide.region_1.8_spmd.clone.clone.sunk | while | flops 1816970880 | bytes 44392472 | solution.py:112
  222.9 119.8 %all-reduce.4.cloned.1.call-done = f32[128,128]{0,1:T(8,128)} async-done(((f32[128,128]{0,1:T(8,128)}), f32[128,128]{0,1:T(8,128)}) %all-reduce.4.cloned.1.call-update) | async-done | bytes 65552 | tf_op jit(solution)/shard_map/while/body/eval_jaxpr/psum | solution.py:13
  344.5 11.7 cholesky.80
  357.4 9.8 custom-call.29
  368.8 5.3 copy.53
  374.1 176.0 %psum.75 = f32[128]{0:T(128)S(1)} all-reduce(f32[128]{0:T(128)S(1)} %fusion.50), channel_id=1, replica_groups=mesh['frames'=2,'prow'=8,'pcol'=8] {'prow','pcol'}, use_global_device_ids=true, to_apply=%region_7.7 | all-reduce | flops 128 | bytes 1024 | tf_op jit(solution)/shard_map/while/body/eval_jaxpr/psum | solution.py:13
  550.1 1.9 broadcast_select_fusion.5
  552.2 1.6 fusion.52
  553.9 66.6 %all-reduce.8.cloned.1.call-done = f32[8,128,128]{2,1,0:T(8,128)} async-done(((f32[8,128,128]{2,1,0:T(8,128)}), f32[8,128,128]{2,1,0:T(8,128)}) %all-reduce.8.cloned.1.call-update) | async-done | bytes 524304 | tf_op jit(solution)/shard_map/while/body/eval_jaxpr/psum | solution.py:13
  620.5 8.2 multiply_subtract_fusion.2
  628.6 1.9 select_dynamic-update-slice_fusion.2
  633.1 5.3 copy.56
  644.7 120.8 %all-reduce.4.cloned.1.call-done = f32[128,128]{0,1:T(8,128)} async-done(((f32[128,128]{0,1:T(8,128)}), f32[128,128]{0,1:T(8,128)}) %all-reduce.4.cloned.1.call-update) | async-done | bytes 65552 | tf_op jit(solution)/shard_map/while/body/eval_jaxpr/psum | solution.py:13
  767.3 11.7 cholesky.80
  780.2 9.8 custom-call.29
  791.6 5.3 copy.53
  796.9 176.0 %psum.75 = f32[128]{0:T(128)S(1)} all-reduce(f32[128]{0:T(128)S(1)} %fusion.50), channel_id=1, replica_groups=mesh['frames'=2,'prow'=8,'pcol'=8] {'prow','pcol'}, use_global_device_ids=true, to_apply=%region_7.7 | all-reduce | flops 128 | bytes 1024 | tf_op jit(solution)/shard_map/while/body/eval_jaxpr/psum | solution.py:13
  973.0 1.9 broadcast_select_fusion.5
  976.7 66.4 %all-reduce.8.cloned.1.call-done = f32[8,128,128]{2,1,0:T(8,128)} async-done(((f32[8,128,128]{2,1,0:T(8,128)}), f32[8,128,128]{2,1,0:T(8,128)}) %all-reduce.8.cloned.1.call-update) | async-done | bytes 524304 | tf_op jit(solution)/shard_map/while/body/eval_jaxpr/psum | solution.py:13
  1043.1 8.2 multiply_subtract_fusion.2
  1051.3 1.9 select_dynamic-update-slice_fusion.2
  1055.7 5.3 copy.56
  1067.4 121.1 %all-reduce.4.cloned.1.call-done = f32[128,128]{0,1:T(8,128)} async-done(((f32[128,128]{0,1:T(8,128)}), f32[128,128]{0,1:T(8,128)}) %all-reduce.4.cloned.1.call-update) | async-done | bytes 65552 | tf_op jit(solution)/shard_map/while/body/eval_jaxpr/psum | solution.py:13
  1190.3 11.7 cholesky.80
  1203.2 9.8 custom-call.29
  1214.6 5.3 copy.53
  1219.9 176.0 %psum.75 = f32[128]{0:T(128)S(1)} all-reduce(f32[128]{0:T(128)S(1)} %fusion.50), channel_id=1, replica_groups=mesh['frames'=2,'prow'=8,'pcol'=8] {'prow','pcol'}, use_global_device_ids=true, to_apply=%region_7.7 | all-reduce | flops 128 | bytes 1024 | tf_op jit(solution)/shard_map/while/body/eval_jaxpr/psum | solution.py:13
  1396.0 1.9 broadcast_select_fusion.5
  1399.7 66.5 %all-reduce.8.cloned.1.call-done = f32[8,128,128]{2,1,0:T(8,128)} async-done(((f32[8,128,128]{2,1,0:T(8,128)}), f32[8,128,128]{2,1,0:T(8,128)}) %all-reduce.8.cloned.1.call-update) | async-done | bytes 524304 | tf_op jit(solution)/shard_map/while/body/eval_jaxpr/psum | solution.py:13
  1466.2 8.2 multiply_subtract_fusion.2
  1474.4 1.9 select_dynamic-update-slice_fusion.2
  1478.8 5.3 copy.56
  1490.4 121.1 %all-reduce.4.cloned.1.call-done = f32[128,128]{0,1:T(8,128)} async-done(((f32[128,128]{0,1:T(8,128)}), f32[128,128]{0,1:T(8,128)}) %all-reduce.4.cloned.1.call-update) | async-done | bytes 65552 | tf_op jit(solution)/shard_map/while/body/eval_jaxpr/psum | solution.py:13
  1613.3 11.7 cholesky.80
  1626.3 9.8 custom-call.29
  1637.6 5.3 copy.53
  1643.0 176.1 %psum.75 = f32[128]{0:T(128)S(1)} all-reduce(f32[128]{0:T(128)S(1)} %fusion.50), channel_id=1, replica_groups=mesh['frames'=2,'prow'=8,'pcol'=8] {'prow','pcol'}, use_global_device_ids=true, to_apply=%region_7.7 | all-reduce | flops 128 | bytes 1024 | tf_op jit(solution)/shard_map/while/body/eval_jaxpr/psum | solution.py:13
  1819.0 1.9 broadcast_select_fusion.5
  1822.8 66.6 %all-reduce.8.cloned.1.call-done = f32[8,128,128]{2,1,0:T(8,128)} async-done(((f32[8,128,128]{2,1,0:T(8,128)}), f32[8,128,128]{2,1,0:T(8,128)}) %all-reduce.8.cloned.1.call-update) | async-done | bytes 524304 | tf_op jit(solution)/shard_map/while/body/eval_jaxpr/psum | solution.py:13
  1889.4 8.2 multiply_subtract_fusion.2
  1897.5 1.9 select_dynamic-update-slice_fusion.2
  1901.9 5.3 copy.56
  1907.3 5.3 copy.44
  (138 shorter events, 53.7 us)
Async XLA Ops:
  7.2 0.7 copy-start
  7.2 3.9 copy-start.3
  7.2 206.6 %all-gather.2.cloned.1.call-start = ((), (), s32[]{:S(2)}) async-start(), calls=%async_computation | async-start | bytes 4227072 | tf_op jit(solution)/shard_map/all_gather | solution.py:52
  9.1 3.6 copy-start.5
  9.1 3.6 copy-start.4
  216.5 126.2 %all-reduce.4.cloned.1.call-start = ((), (), s32[]{:S(2)}) async-start(), calls=%async_computation.1 | async-start | bytes 131072 | tf_op jit(solution)/shard_map/while/body/eval_jaxpr/psum | solution.py:13
  220.9 329.2 %all-reduce.6.cloned.1.call-start = ((), (), s32[]{:S(2)}) async-start(), calls=%async_computation.2 | async-start | bytes 1048576 | tf_op jit(solution)/shard_map/while/body/eval_jaxpr/psum | solution.py:13
  368.7 251.8 %all-reduce.8.cloned.1.call-start = ((), (), s32[]{:S(2)}) async-start(), calls=%async_computation.3 | async-start | bytes 1048576 | tf_op jit(solution)/shard_map/while/body/eval_jaxpr/psum | solution.py:13
  620.5 11.1 copy-start.1
  638.4 127.1 %all-reduce.4.cloned.1.call-start = ((), (), s32[]{:S(2)}) async-start(), calls=%async_computation.1 | async-start | bytes 131072 | tf_op jit(solution)/shard_map/while/body/eval_jaxpr/psum | solution.py:13
  642.8 330.2 %all-reduce.6.cloned.1.call-start = ((), (), s32[]{:S(2)}) async-start(), calls=%async_computation.2 | async-start | bytes 1048576 | tf_op jit(solution)/shard_map/while/body/eval_jaxpr/psum | solution.py:13
  791.5 251.6 %all-reduce.8.cloned.1.call-start = ((), (), s32[]{:S(2)}) async-start(), calls=%async_computation.3 | async-start | bytes 1048576 | tf_op jit(solution)/shard_map/while/body/eval_jaxpr/psum | solution.py:13
  1043.1 11.1 copy-start.1
  1061.1 127.4 %all-reduce.4.cloned.1.call-start = ((), (), s32[]{:S(2)}) async-start(), calls=%async_computation.1 | async-start | bytes 131072 | tf_op jit(solution)/shard_map/while/body/eval_jaxpr/psum | solution.py:13
  1065.4 330.5 %all-reduce.6.cloned.1.call-start = ((), (), s32[]{:S(2)}) async-start(), calls=%async_computation.2 | async-start | bytes 1048576 | tf_op jit(solution)/shard_map/while/body/eval_jaxpr/psum | solution.py:13
  1214.5 251.7 %all-reduce.8.cloned.1.call-start = ((), (), s32[]{:S(2)}) async-start(), calls=%async_computation.3 | async-start | bytes 1048576 | tf_op jit(solution)/shard_map/while/body/eval_jaxpr/psum | solution.py:13
  1466.2 11.1 copy-start.1
  1484.1 127.4 %all-reduce.4.cloned.1.call-start = ((), (), s32[]{:S(2)}) async-start(), calls=%async_computation.1 | async-start | bytes 131072 | tf_op jit(solution)/shard_map/while/body/eval_jaxpr/psum | solution.py:13
  1488.5 330.5 %all-reduce.6.cloned.1.call-start = ((), (), s32[]{:S(2)}) async-start(), calls=%async_computation.2 | async-start | bytes 1048576 | tf_op jit(solution)/shard_map/while/body/eval_jaxpr/psum | solution.py:13
  1637.5 251.8 %all-reduce.8.cloned.1.call-start = ((), (), s32[]{:S(2)}) async-start(), calls=%async_computation.3 | async-start | bytes 1048576 | tf_op jit(solution)/shard_map/while/body/eval_jaxpr/psum | solution.py:13
  1889.4 11.1 copy-start.1
  1907.3 5.3 copy-start.2
Sparse Core Ops, SparseCore 0:
  12.7 201.0 all-gather.1
  222.6 120.0 all-reduce.3
  368.8 83.5 all-reduce.5
  552.2 68.2 all-reduce.7
  644.2 121.2 all-reduce.3
  791.6 83.5 all-reduce.5
  975.0 68.0 all-reduce.7
  1067.2 121.2 all-reduce.3
  1214.6 83.5 all-reduce.5
  1398.0 68.1 all-reduce.7
  1490.2 121.2 all-reduce.3
  1637.7 83.5 all-reduce.5
  1821.1 68.2 all-reduce.7
